TPU v7x, 256 devices: a whole 4x4x8 slice. The times are simulated.
256 devices in a mesh: grp: 8 (over y, x_hi), row: 32 (over z, x_lo, core).
Axes of the slice: x: 4 (x_hi: 2, x_lo: 2; x = x_hi * 2 + x_lo), y: 4, z: 8, core: 2. Of those that a mesh axis runs over, the one named last changes fastest.
Arguments:
- features: float32 [32768, 256], P(('grp', 'row')), may hold values from -6 to 6
- adjacency_tiles: float32 [128, 8, 6, 256, 256], P('row', 'grp'), may hold values from -0.078125 to 0.078125
- tile_cols: int32 [128, 8, 6], P('row', 'grp'), may hold values from 0 to 15, as said below
- tile_count: int32 [128, 8], P('row', 'grp'), may hold values from 1 to 6, as said below
- weight: float32 [256, 256], replicated, may hold values from -0.375 to 0.375
- layer_bias: float32 [256], replicated, may hold values from -3 to 3
- cotangent: float32 [32768, 256], P('row'), may hold values from -6 to 6
Outputs:
- hidden_out: float32 [32768, 256], P('row')
- grad_features: float32 [32768, 256], P(('grp', 'row'))
- grad_weight: float32 [256, 256], replicated
- grad_bias: float32 [256], replicated
Inputs may be any that keep to these rules, and one draw needn't show every extreme that they name: `tile_cols`: for each block row and column range the 6 slots name distinct column blocks. `tile_count`: in every column range some block row has all 6 slots live.
All inputs are finite; a program needn't handle non-finite values.
Results may differ from a plain program's by a relative error of at most 0.0003.
Values sent between devices are 32-bit elements; how exact they have to be, the bound alone decides.
A program may use at most 128 MiB of HBM per device.

v0:
```python
import jax
import jax.numpy as jnp
from jax import lax
from jax.sharding import PartitionSpec as P


def activate(summed, upstream, weight, layer_bias):
    highest = lax.Precision.HIGHEST
    preact = jnp.dot(summed, weight, precision=highest) + layer_bias
    sigma = jax.nn.sigmoid(preact)
    grad_pre = upstream * sigma * (1.0 + preact * (1.0 - sigma))
    return (preact * sigma, grad_pre)


def on_device(features, adjacency_tiles, tile_cols, tile_count, weight, layer_bias, cotangent):
    highest = lax.Precision.HIGHEST
    block_rows, _, slot_count, tile_size, _ = adjacency_tiles.shape
    panel = lax.all_gather(features, "row", axis=0, tiled=True)
    width = panel.shape[1]
    blocks = panel.shape[0] // tile_size
    slots = lax.broadcasted_iota(jnp.int32, (block_rows, slot_count), 1)
    live = (slots < tile_count).astype(jnp.float32)
    block_ids = lax.broadcasted_iota(jnp.int32, (block_rows, slot_count, blocks), 2)
    picks = (tile_cols[:, 0, :, None] == block_ids).astype(jnp.float32) * live[:, :, None]
    local_tiles = adjacency_tiles[:, 0]
    chosen = jnp.einsum(
        "btc,cjf->btjf", picks, panel.reshape(blocks, tile_size, width), precision=highest
    )
    partial_rows = jnp.einsum("btij,btjf->bif", local_tiles, chosen, precision=highest).reshape(
        block_rows * tile_size, width
    )
    scaling = 1.0 / float(block_rows * tile_size * lax.axis_size("row")) ** 0.5
    summed = lax.psum(partial_rows, "grp")
    layer_out, grad_pre = activate(summed, cotangent, weight, layer_bias)
    weight_term = jnp.dot(summed.T, grad_pre, precision=highest) * scaling
    bias_term = jnp.sum(grad_pre, axis=0) * scaling
    grad_weight, grad_bias = lax.psum((weight_term, bias_term), "row")
    backward = jnp.dot(grad_pre, weight.T, precision=highest)
    spread = jnp.einsum(
        "btij,bif->btjf",
        local_tiles,
        backward.reshape(block_rows, tile_size, width),
        precision=highest,
    )
    grad_panel = jnp.einsum("btc,btjf->cjf", picks, spread, precision=highest).reshape(
        blocks * tile_size, width
    )
    grad_owned = lax.psum_scatter(grad_panel, "row", scatter_dimension=0, tiled=True)
    return (layer_out, grad_owned, grad_weight, grad_bias)


def solution(mesh):
    return jax.shard_map(
        on_device,
        mesh=mesh,
        in_specs=(
            P(("grp", "row"), None),
            P("row", "grp", None, None, None),
            P("row", "grp", None),
            P("row", "grp"),
            P(),
            P(),
            P("row", None),
        ),
        out_specs=(P("row", None), P(("grp", "row"), None), P(), P()),
        check_vma=False,
    )
```

profile of v0, /device:TPU:16, one launch (start us, length us, event | category | flops | bytes accessed | tf_op | source)
XLA Modules:
  0.0 565.5 jit_solution(5792356195475707266)
XLA Ops:
  7.2 0.0 copy-start
  7.2 0.0 all-gather.2.cloned.1.call-start
  7.2 0.0 slice-start
  7.2 0.7 all-gather.2.cloned.1.call-update
  7.9 0.0 all-reduce.3.cloned.1.call-start
  8.0 0.7 fusion.19
  8.7 70.5 %all-gather.2.cloned.1.call-done = f32[4096,256]{1,0:T(8,128)} async-done(((f32[128,256]{1,0:T(8,128)}), f32[4096,256]{1,0:T(8,128)}) %all-gather.2.cloned.1.call-update) | async-done | bytes 4194320 | tf_op jit(solution)/shard_map/all_gather | solution.py:18
  79.2 0.0 slice-start.1
  79.2 11.8 %fusion.7 = f32[4,6,256,256]{3,1,2,0:T(8,128)S(1)} fusion(f32[16,256,256,1]{2,1,0,3:T(8,128)} %bitcast.47, f32[4,6]{1,0:T(4,128)S(1)} %fusion.19, s32[4,6]{1,0:T(4,128)} %bitcast.50), kind=kOutput, calls=%fused_computation.7 | convolution fusion | flops 301990656 | bytes 10485952 | tf_op jit(solution)/shard_map/btc,cjf->btjf/dot_general | solution.py:26
  91.0 0.0 slice-done
  91.0 0.0 slice-done.1
  91.0 0.0 copy-start.3
  91.1 0.0 copy-start.4
  91.1 9.5 %fusion.4 = f32[4,256,256,1]{1,2,3,0:T(8,128)} fusion(f32[4,1,6,256,256]{4,3,2,1,0:T(8,128)S(1)} %bitcast.45, f32[4,6,256,256]{3,1,2,0:T(8,128)S(1)} %fusion.7), kind=kOutput, calls=%fused_computation.4 | convolution fusion | flops 4831838208 | bytes 13631488 | tf_op jit(solution)/shard_map/btij,btjf->bif/dot_general | solution.py:29
  100.6 0.0 all-reduce.3.cloned.1.call-update
  100.6 0.3 all-reduce.5.cloned.1.call-start
  100.9 93.2 %all-reduce.3.cloned.1.call-done = f32[1024,256]{1,0:T(8,128)} async-done(((f32[1024,256]{1,0:T(8,128)}), f32[1024,256]{1,0:T(8,128)}) %all-reduce.3.cloned.1.call-update) | async-done | bytes 1048592 | tf_op jit(solution)/shard_map/psum | solution.py:33
  194.0 0.0 copy-done
  194.0 0.0 copy-done.3
  194.0 0.0 copy-done.4
  194.0 0.0 copy-start.1
  194.0 3.6 fusion.22
  197.6 1.0 fusion.23
  198.6 0.0 copy-done.1
  198.6 2.5 convolution_multiply_fusion
  201.2 0.0 all-reduce.5.cloned.1.call-update
  201.2 0.0 reduce-scatter.2.cloned.1.call-start
  201.2 11.8 %fusion.2 = f32[4,256,6,256]{3,1,2,0:T(8,128)} fusion(f32[4,256,256,1]{2,1,3,0:T(8,128)S(1)} %bitcast.48, f32[4,1,6,256,256]{4,3,2,1,0:T(8,128)} %param.8), kind=kOutput, calls=%fused_computation.2 | convolution fusion | flops 4831838208 | bytes 13631488 | tf_op jit(solution)/shard_map/btij,bif->btjf/dot_general | solution.py:39
  213.1 0.0 copy-start.2
  213.1 9.4 %copy.17 = f32[4,256,6,256]{1,2,0,3:T(8,128)} copy(f32[4,256,6,256]{3,1,2,0:T(8,128)} %fusion.2) | data formatting | bytes 12582912 | tf_op jit(solution)/shard_map/btij,bif->btjf/dot_general | solution.py:39
  222.5 0.0 copy-done.2
  222.5 9.3 %fusion.9 = f32[16,256,256]{2,0,1:T(8,128)S(1)} fusion(f32[4,256,6,256]{1,2,0,3:T(8,128)} %copy.17, f32[4,6]{1,0:T(4,128)S(1)} %fusion.19, s32[4,6]{1,0:T(4,128)S(1)} %bitcast.51), kind=kOutput, calls=%fused_computation.9 | convolution fusion | flops 301990656 | bytes 10485952 | tf_op jit(solution)/shard_map/btc,btjf->cjf/dot_general | solution.py:45
  231.8 4.4 copy.11
  236.1 0.0 reduce-scatter.2.cloned.1.call-update
  236.2 53.5 %psum.23 = f32[256]{0:T(256)} all-reduce(f32[256]{0:T(256)S(1)} %broadcast_multiply_fusion), channel_id=1, replica_groups=mesh['grp'=8,'row'=32] {'row'}, use_global_device_ids=true, to_apply=%region_4.0 | all-reduce | flops 256 | bytes 2048 | tf_op jit(solution)/shard_map/psum | solution.py:37
  289.7 138.6 %all-reduce.5.cloned.1.call-done = f32[256,256]{1,0:T(8,128)} async-done(((f32[256,256]{1,0:T(8,128)}), f32[256,256]{1,0:T(8,128)}) %all-reduce.5.cloned.1.call-update) | async-done | bytes 262160 | tf_op jit(solution)/shard_map/psum | solution.py:37
  428.3 128.9 %reduce-scatter.2.cloned.1.call-done = f32[128,256]{1,0:T(8,128)} async-done(((f32[4096,256]{1,0:T(8,128)}), f32[128,256]{1,0:T(8,128)}) %reduce-scatter.2.cloned.1.call-update) | async-done | bytes 131088 | tf_op jit(solution)/shard_map/reduce_scatter | solution.py:48
  557.3 1.7 copy.25
  (2 shorter events, 0.0 us)
Async XLA Ops:
  7.2 186.9 %copy-start = (f32[256,256]{1,0:T(8,128)S(1)}, f32[256,256]{1,0:T(8,128)}, u32[]{:S(2)}) copy-start(f32[256,256]{1,0:T(8,128)} %param.11) | copy-start | bytes 786436
  7.2 72.0 %all-gather.2.cloned.1.call-start = ((), (), s32[]{:S(2)}) async-start(), calls=%async_computation.1 | async-start | bytes 4325376 | tf_op jit(solution)/shard_map/all_gather | solution.py:18
  7.2 83.8 %slice-start = ((s8[6291456]{0:T(1024)(128)(4,1)}), s8[2097152]{0:T(1024)(128)(4,1)S(1)}, s32[]{:S(2)}) async-start(s8[6291456]{0:T(1024)(128)(4,1)} %bitcast.44), calls=%async_computation.5 | async-start | bytes 4194304
  7.9 186.1 %all-reduce.3.cloned.1.call-start = ((), (), s32[]{:S(2)}) async-start(), calls=%async_computation.2 | async-start | bytes 2097152 | tf_op jit(solution)/shard_map/psum | solution.py:33
  79.2 11.9 %slice-start.1 = ((s8[6291456]{0:T(1024)(128)(4,1)}), s8[4194304]{0:T(1024)(128)(4,1)S(1)}, s32[]{:S(2)}) async-start(s8[6291456]{0:T(1024)(128)(4,1)} %bitcast.44), calls=%async_computation.6 | async-start | bytes 8388608
  91.0 103.0 %copy-start.3 = (f32[1024,256]{1,0:T(8,128)S(1)}, f32[1024,256]{1,0:T(8,128)}, u32[]{:S(2)}) copy-start(f32[1024,256]{1,0:T(8,128)} %param.13) | copy-start | bytes 3145732
  91.1 103.0 %copy-start.4 = (f32[256]{0:T(256)S(1)}, f32[256]{0:T(256)}, u32[]{:S(2)}) copy-start(f32[256]{0:T(256)} %param.12) | copy-start | bytes 3076
  100.6 327.7 %all-reduce.5.cloned.1.call-start = ((), (), s32[]{:S(2)}) async-start(), calls=%async_computation.4 | async-start | bytes 524288 | tf_op jit(solution)/shard_map/psum | solution.py:37
  194.0 4.6 copy-start.1
  201.2 356.1 %reduce-scatter.2.cloned.1.call-start = ((), (), s32[]{:S(2)}) async-start(), calls=%async_computation.3 | async-start | bytes 4325376 | tf_op jit(solution)/shard_map/reduce_scatter | solution.py:48
  213.1 9.4 %copy-start.2 = (s32[4,1,6]{2,1,0:T(1,128)S(1)}, s32[4,1,6]{2,1,0:T(1,128)}, u32[]{:S(2)}) copy-start(s32[4,1,6]{2,1,0:T(1,128)} %param.9) | copy-start | bytes 292
Sparse Core Ops, SparseCore 0:
  9.8 69.2 all-gather.1
  100.7 93.2 all-reduce.2
  201.3 226.9 all-reduce.4
  431.3 125.9 reduce-scatter.1
where the time goes:
time: 566 us; the launch traced here: 565 us
  waiting for transfers between devices  432 us (76%)
  blocking collectives  53.5 us (9%)
  matrix products  49.5 us (9%)
  local copies, waits for them, and re-layouts  15.5 us (3%)
  between operations  13.9 us (2%)
    psum x1, waiting for transfers between devices, on_device(): grad_weight, grad_bias = lax.psum((weight_term, bias_term), 'row')  139 us
    reduce_scatter x1, waiting for transfers between devices, on_device(): lax.psum_scatter(grad_panel, 'row', scatter_dimension=0, tiled=True)  129 us
    psum x1, waiting for transfers between devices, on_device(): summed = lax.psum(partial_rows, 'grp')  93.2 us
    all_gather x1, waiting for transfers between devices, on_device(): panel = lax.all_gather(features, 'row', axis=0, tiled=True)  70.5 us
    psum x1, blocking collectives, on_device(): grad_weight, grad_bias = lax.psum((weight_term, bias_term), 'row')  53.5 us
    dot_general x1, matrix products, on_device(): jnp.einsum('btc,cjf->btjf', picks, panel.reshape(blocks, tile_size, width...  11.8 us
    dot_general x1, matrix products, on_device(): jnp.einsum('btij,bif->btjf', local_tiles, backward.reshape(block_rows, ti...  11.8 us
  transfers between devices with their start and end apart: 4, of which 4 were waited for; matrix products, arithmetic and copies ran while one was open for 6% of the time, Pallas kernels for 0%

commit v1 on v0

--- a/solution.py
+++ b/solution.py
@@ -30,7 +30,7 @@
         block_rows * tile_size, width
     )
     scaling = 1.0 / float(block_rows * tile_size * lax.axis_size("row")) ** 0.5
-    summed = lax.psum(partial_rows, "grp")
+    summed = jnp.sum(lax.all_gather(partial_rows, "grp"), axis=0)
     layer_out, grad_pre = activate(summed, cotangent, weight, layer_bias)
     weight_term = jnp.dot(summed.T, grad_pre, precision=highest) * scaling
     bias_term = jnp.sum(grad_pre, axis=0) * scaling

time: 566 us -> 584 us (1.032)
  waiting for transfers between devices: 432 us -> 445 us
    all_gather x0 -> x1, waiting for transfers between devices: none -> 110 us  [on_device(): summed = jnp.sum(lax.all_gather(partial_rows, 'grp'), axis=0)]
    psum x1 -> x0, waiting for transfers between devices: 93.2 us -> none  [on_device(): summed = lax.psum(partial_rows, 'grp')]
where the time goes in v1:
time: 584 us
  waiting for transfers between devices  445 us (76%)
  blocking collectives  55.6 us (10%)
  matrix products  48.3 us (8%)
  local copies, waits for them, and re-layouts  15.5 us (3%)
  between operations  13.9 us (2%)
    psum x1, waiting for transfers between devices, on_device(): grad_weight, grad_bias = lax.psum((weight_term, bias_term), 'row')  135 us
    reduce_scatter x1, waiting for transfers between devices, on_device(): lax.psum_scatter(grad_panel, 'row', scatter_dimension=0, tiled=True)  129 us
    all_gather x1, waiting for transfers between devices, on_device(): summed = jnp.sum(lax.all_gather(partial_rows, 'grp'), axis=0)  110 us
    all_gather x1, waiting for transfers between devices, on_device(): panel = lax.all_gather(features, 'row', axis=0, tiled=True)  70.5 us
    psum x1, blocking collectives, on_device(): grad_weight, grad_bias = lax.psum((weight_term, bias_term), 'row')  55.6 us
    dot_general x1, matrix products, on_device(): jnp.einsum('btij,bif->btjf', local_tiles, backward.reshape(block_rows, ti...  11.9 us
    dot_general x1, matrix products, on_device(): jnp.einsum('btc,cjf->btjf', picks, panel.reshape(blocks, tile_size, width...  11.8 us
  transfers between devices with their start and end apart: 4, of which 4 were waited for; matrix products, arithmetic and copies ran while one was open for 6% of the time, Pallas kernels for 0%

profile of v1, /device:TPU:16, one launch (start us, length us, event | category | flops | bytes accessed | tf_op | source)
XLA Modules:
  0.0 583.7 jit_solution(18388002900889105483)
XLA Ops:
  7.2 0.0 copy-start
  7.2 0.0 all-gather.3.cloned.1.call-start
  7.2 0.0 slice-start
  7.2 0.7 all-gather.3.cloned.1.call-update
  7.9 0.0 all-gather.5.cloned.1.call-start
  8.0 0.7 fusion.18
  8.7 70.5 %all-gather.3.cloned.1.call-done = f32[4096,256]{1,0:T(8,128)} async-done(((f32[128,256]{1,0:T(8,128)}), f32[4096,256]{1,0:T(8,128)}) %all-gather.3.cloned.1.call-update) | async-done | bytes 4194320 | tf_op jit(solution)/shard_map/all_gather | solution.py:18
  79.2 0.0 slice-start.1
  79.2 11.8 %fusion.5 = f32[4,6,256,256]{3,1,2,0:T(8,128)S(1)} fusion(f32[16,256,256]{2,1,0:T(8,128)} %bitcast.48, f32[4,6]{1,0:T(4,128)S(1)} %fusion.18, s32[4,6]{1,0:T(4,128)} %bitcast.51), kind=kOutput, calls=%fused_computation.5 | convolution fusion | flops 301990656 | bytes 10485952 | tf_op jit(solution)/shard_map/btc,cjf->btjf/dot_general | solution.py:26
  91.0 0.0 slice-done
  91.0 0.0 slice-done.1
  91.0 9.5 %fusion.2 = f32[4,256,256,1]{1,2,3,0:T(8,128)} fusion(f32[4,1,6,256,256]{4,3,2,1,0:T(8,128)S(1)} %bitcast.46, f32[4,6,256,256]{3,1,2,0:T(8,128)S(1)} %fusion.5), kind=kOutput, calls=%fused_computation.2 | convolution fusion | flops 4831838208 | bytes 13631488 | tf_op jit(solution)/shard_map/btij,btjf->bif/dot_general | solution.py:29
  100.6 0.0 copy-start.2
  100.6 0.0 copy-start.3
  100.6 0.0 all-gather.5.cloned.1.call-update
  100.6 0.3 all-reduce.2.cloned.1.call-start
  100.9 109.9 %all-gather.5.cloned.1.call-done = f32[8,1024,256]{2,1,0:T(8,128)} async-done(((f32[1,1024,256]{2,1,0:T(8,128)}), f32[8,1024,256]{2,1,0:T(8,128)}) %all-gather.5.cloned.1.call-update) | async-done | bytes 8388624 | tf_op jit(solution)/shard_map/all_gather | solution.py:33
  210.7 4.1 reduce_sum.18
  214.8 0.0 copy-done
  214.8 0.0 copy-done.2
  214.8 0.0 copy-done.3
  214.8 2.3 fusion.21
  217.1 2.5 convolution_multiply_fusion
  219.6 1.0 fusion.22
  220.6 0.0 all-reduce.2.cloned.1.call-update
  220.7 0.3 reduce-scatter.2.cloned.1.call-start
  221.0 11.9 %fusion.8 = f32[4,6,256,256]{2,3,1,0:T(8,128)} fusion(f32[4,256,256,1]{2,1,3,0:T(8,128)S(1)} %bitcast.50, f32[4,1,6,256,256]{4,3,2,1,0:T(8,128)} %param.8), kind=kOutput, calls=%fused_computation.8 | convolution fusion | flops 4831838208 | bytes 13631488 | tf_op jit(solution)/shard_map/btij,bif->btjf/dot_general | solution.py:39
  232.8 0.0 copy-start.1
  232.8 9.4 %copy.19 = f32[4,6,256,256]{3,1,0,2:T(8,128)} copy(f32[4,6,256,256]{2,3,1,0:T(8,128)} %fusion.8) | data formatting | bytes 12582912 | tf_op jit(solution)/shard_map/btij,bif->btjf/dot_general | solution.py:39
  242.3 0.0 copy-done.1
  242.3 9.3 %convolution_bitcast_fusion = f32[16,256,256]{2,0,1:T(8,128)S(1)} fusion(f32[4,6,256,256]{3,1,0,2:T(8,128)} %copy.19, f32[4,6]{1,0:T(4,128)S(1)} %fusion.18, s32[4,6]{1,0:T(4,128)S(1)} %bitcast.52), kind=kOutput, calls=%fused_computation.9 | convolution fusion | flops 301990656 | bytes 10485952 | tf_op jit(solution)/shard_map/btc,btjf->cjf/dot_general | solution.py:45
  251.6 4.4 copy.20
  255.9 0.0 reduce-scatter.2.cloned.1.call-update
  256.0 55.6 %psum.15 = f32[256]{0:T(256)} all-reduce(f32[256]{0:T(256)S(1)} %broadcast_multiply_fusion), channel_id=1, replica_groups=mesh['grp'=8,'row'=32] {'row'}, use_global_device_ids=true, to_apply=%region_4.0 | all-reduce | flops 256 | bytes 2048 | tf_op jit(solution)/shard_map/psum | solution.py:37
  311.5 135.0 %all-reduce.2.cloned.1.call-done = f32[256,256]{1,0:T(8,128)} async-done(((f32[256,256]{1,0:T(8,128)}), f32[256,256]{1,0:T(8,128)}) %all-reduce.2.cloned.1.call-update) | async-done | bytes 262160 | tf_op jit(solution)/shard_map/psum | solution.py:37
  446.6 128.9 %reduce-scatter.2.cloned.1.call-done = f32[128,256]{1,0:T(8,128)} async-done(((f32[4096,256]{1,0:T(8,128)}), f32[128,256]{1,0:T(8,128)}) %reduce-scatter.2.cloned.1.call-update) | async-done | bytes 131088 | tf_op jit(solution)/shard_map/reduce_scatter | solution.py:48
  575.5 1.7 copy.34
  (2 shorter events, 0.0 us)
Async XLA Ops:
  7.2 207.6 %copy-start = (f32[256,256]{1,0:T(8,128)S(1)}, f32[256,256]{1,0:T(8,128)}, u32[]{:S(2)}) copy-start(f32[256,256]{1,0:T(8,128)} %param.11) | copy-start | bytes 786436
  7.2 72.0 %all-gather.3.cloned.1.call-start = ((), (), s32[]{:S(2)}) async-start(), calls=%async_computation.1 | async-start | bytes 4325376 | tf_op jit(solution)/shard_map/all_gather | solution.py:18
  7.2 83.8 %slice-start = ((s8[6291456]{0:T(1024)(128)(4,1)}), s8[2097152]{0:T(1024)(128)(4,1)S(1)}, s32[]{:S(2)}) async-start(s8[6291456]{0:T(1024)(128)(4,1)} %bitcast.45), calls=%async_computation.5 | async-start | bytes 4194304
  7.9 202.8 %all-gather.5.cloned.1.call-start = ((), (), s32[]{:S(2)}) async-start(), calls=%async_computation.2 | async-start | bytes 9437184 | tf_op jit(solution)/shard_map/all_gather | solution.py:33
  79.2 11.9 %slice-start.1 = ((s8[6291456]{0:T(1024)(128)(4,1)}), s8[4194304]{0:T(1024)(128)(4,1)S(1)}, s32[]{:S(2)}) async-start(s8[6291456]{0:T(1024)(128)(4,1)} %bitcast.45), calls=%async_computation.6 | async-start | bytes 8388608
  100.6 114.2 %copy-start.2 = (f32[1024,256]{1,0:T(8,128)S(1)}, f32[1024,256]{1,0:T(8,128)}, u32[]{:S(2)}) copy-start(f32[1024,256]{1,0:T(8,128)} %param.13) | copy-start | bytes 3145732
  100.6 114.2 %copy-start.3 = (f32[256]{0:T(256)S(1)}, f32[256]{0:T(256)}, u32[]{:S(2)}) copy-start(f32[256]{0:T(256)} %param.12) | copy-start | bytes 3076
  100.6 346.0 %all-reduce.2.cloned.1.call-start = ((), (), s32[]{:S(2)}) async-start(), calls=%async_computation.4 | async-start | bytes 524288 | tf_op jit(solution)/shard_map/psum | solution.py:37
  220.7 354.9 %reduce-scatter.2.cloned.1.call-start = ((), (), s32[]{:S(2)}) async-start(), calls=%async_computation.3 | async-start | bytes 4325376 | tf_op jit(solution)/shard_map/reduce_scatter | solution.py:48
  232.8 9.4 %copy-start.1 = (s32[4,1,6]{2,1,0:T(1,128)S(1)}, s32[4,1,6]{2,1,0:T(1,128)}, u32[]{:S(2)}) copy-start(s32[4,1,6]{2,1,0:T(1,128)} %param.9) | copy-start | bytes 292
Sparse Core Ops, SparseCore 0:
  9.8 69.2 all-gather.2
  100.7 109.9 all-gather.4
  220.8 225.7 all-reduce.1
  449.5 125.9 reduce-scatter.1
